TPU v7x, 32 devices: a whole 2x2x4 slice. The times are simulated.
32 devices in a mesh: pulse: 4 (over z), tile: 8 (over y, x, core).
Axes of the slice: x: 2, y: 2, z: 4, core: 2. Of those that a mesh axis runs over, the one named last changes fastest.
Arguments:
- raw: bfloat16 [2, 128, 2048], P(None, ('pulse', 'tile')), may hold values from -6 to 6
- filt: bfloat16 [2, 1024, 2048], replicated, may hold values from -0.125 to 0.125
- range_off: int32 [128], P(('pulse', 'tile')), may hold values from 0 to 1024
- fine: int32 [128], P(('pulse', 'tile')), may hold values from 0 to 3
- dop: int32 [128], P(('pulse', 'tile')), may hold values from 0 to 511
- pulse_order: int32 [32, 4], P(('pulse', 'tile')), may hold values from 0 to 3, each once within a row
- band_idx: int32 [8, 128], P(None, ('pulse', 'tile')), may hold values from 0 to 1023
Outputs:
- image: bfloat16 [2, 512, 32768], P(None, 'pulse', 'tile')
Inputs may be any that keep to these rules, and one draw needn't show every extreme that they name: `pulse_order`: each row is a permutation of 0 .. 3.
All inputs are finite; a program needn't handle non-finite values.
Results may differ from a plain program's by a relative error of at most 0.0065.
Values may be sent and summed in bfloat16 or wider, within the bound.
A program may use at most 192 MiB of HBM per device.

v0:
```python
import functools

import jax
import jax.numpy as jnp
from jax import lax
from jax.experimental import pallas as pl
from jax.experimental.pallas import tpu as pltpu
from jax.sharding import PartitionSpec as P

F32 = jnp.float32
BF16 = jnp.bfloat16
MESH = pl.DeviceIdType.MESH
LANES = 128
DOP_SPLIT = 32
VMEM_LIMIT = 60 * 1024 * 1024


def spread(meta, field, rows8, n_rows):
    lane = lax.broadcasted_iota(jnp.int32, (meta.shape[1], n_rows), 0)
    col = lax.broadcasted_iota(jnp.int32, (meta.shape[1], n_rows), 1)
    pick = (lane == field * rows8 + col % rows8).astype(F32).astype(BF16)
    wide = jnp.dot(meta, pick, preferred_element_type=F32)
    owner = lax.broadcasted_iota(jnp.int32, wide.shape, 0)
    column = lax.broadcasted_iota(jnp.int32, wide.shape, 1)
    return jnp.sum(jnp.where(owner == column // rows8, wide, 0.0), axis=0, keepdims=True)


def thirds(x):
    a = x.astype(BF16)
    rest = x - a.astype(F32)
    b = rest.astype(BF16)
    return [a, b, (rest - b.astype(F32)).astype(BF16)]


def swap_parts(v, part1, p_dev):
    n = v.shape[-1]
    return jnp.where(part1, pltpu.roll(v, p_dev, 1), pltpu.roll(v, n - p_dev, 1))


def focus_kernel(
    n_pulse, n_tile, r_dev,
    off_ref, fine_ref, dop_ref, order_ref, idx_ref, raw_ref, filt_ref,
    left_ref, samp_out,
    samp_ref, o_sem, bands_ref, up_ref, win_ref, meta_ref, scal_ref, filt_buf, x_ref, prof_ref, cut_ref, out_buf, g_ref, got_ref,
    f_sem, s_sem, z_send, z_recv, t_send, t_recv, p_send, p_recv, g_send, g_recv,
):
    me_p = lax.axis_index("pulse")
    me_t = lax.axis_index("tile")
    half = n_tile // 2
    core = me_t % 2
    chip = me_t // 2
    partner = chip * 2 + (1 - core)
    p_dev = raw_ref.shape[1]
    steps = order_ref.shape[1]
    raw_len = raw_ref.shape[2]
    win = x_ref.shape[2]
    rows = x_ref.shape[1]
    rows8 = 2 * p_dev
    n_dev = n_pulse * half
    n_rows = 2 * rows
    chunks, chunk = filt_buf.shape[0], filt_buf.shape[3]
    stride = prof_ref.shape[0] // rows
    band = bands_ref.shape[3]
    pieces = band // LANES

    def pulse_peer(d):
        return (lax.rem(me_p + d, n_pulse), me_t)

    def tile_peer(d):
        return (me_p, lax.rem(chip + d, half) * 2 + core)

    def any_tile(d):
        return (me_p, lax.rem(me_t + d, n_tile))

    barrier = pltpu.get_barrier_semaphore()
    for d in range(1, n_pulse):
        pl.semaphore_signal(barrier, 1, device_id=pulse_peer(d), device_id_type=MESH)
    for d in range(1, n_tile):
        pl.semaphore_signal(barrier, 1, device_id=any_tile(d), device_id_type=MESH)

    def load_filter(n):
        return pltpu.make_async_copy(
            filt_ref.at[:, :, pl.ds(n * chunk, chunk)], filt_buf.at[n], f_sem.at[n]
        )

    for n in range(chunks):
        load_filter(n).start()

    raw = jnp.concatenate([raw_ref[0].astype(F32), raw_ref[1].astype(F32)], 0)
    row = lax.broadcasted_iota(jnp.int32, (rows8, win), 0)
    cut = jnp.zeros((rows8, win), F32)
    for p in range(p_dev):
        off = off_ref[p]
        shift = jnp.where(off == 0, 0, raw_len - off)
        turned = pltpu.roll(raw, shift, 1)[:, :win]
        cut = jnp.where(row % p_dev == p, turned, cut)
    mine = me_p * half + chip
    win_ref[mine] = cut.astype(BF16)
    lane = lax.broadcasted_iota(jnp.int32, meta_ref.shape[2:], 1)
    line = jnp.zeros(meta_ref.shape[2:], jnp.int32)
    for p in range(p_dev):
        pulse_lane = (lane < 4 * rows8) & (lane % p_dev == p)
        line = jnp.where(pulse_lane & (lane // rows8 == 1), fine_ref[p], line)
        line = jnp.where(pulse_lane & (lane // rows8 == 2), dop_ref[p] % DOP_SPLIT, line)
        line = jnp.where(pulse_lane & (lane // rows8 == 3), dop_ref[p] // DOP_SPLIT, line)
        line = jnp.where((lane < rows8) & (lane % p_dev == order_ref[0, p]), p, line)
        for t in range(n_tile):
            line = jnp.where(lane == 4 * rows8 + t * p_dev + p, idx_ref[p, t], line)
    meta_ref[core, mine] = line
    j = lax.broadcasted_iota(jnp.int32, up_ref.shape, 0)
    c = lax.broadcasted_iota(jnp.int32, up_ref.shape, 1)
    w = (c % 4).astype(F32) * 0.25
    up = jnp.where(j < LANES, 1.0 - w, w)
    up_ref[...] = jnp.where(j % LANES == c // 4, up, 0.0).astype(BF16)
    pl.semaphore_wait(barrier, n_pulse - 1 + n_tile - 1)

    def copies(slot, send, recv, at, target):
        return [
            pltpu.make_async_remote_copy(
                src_ref=ref, dst_ref=ref, send_sem=send.at[(a,) + at], recv_sem=recv.at[(a,) + at],
                device_id=target, device_id_type=MESH,
            )
            for a, ref in enumerate((win_ref.at[slot], meta_ref.at[core, slot]))
        ]

    started = []

    def send(*args):
        for c in copies(*args):
            c.start()
            started.append(c)

    def arrive(*args):
        for c in copies(*args):
            c.wait_recv()

    for d in reversed(range(1, n_pulse)):
        send(mine, z_send, z_recv, (d,), pulse_peer(d))
    for dp in range(n_pulse):
        slot = lax.rem(me_p + n_pulse - dp, n_pulse) * half + chip
        if dp:
            arrive(slot, z_send, z_recv, (dp,), pulse_peer(dp))
        for dt in reversed(range(1, half)):
            send(slot, t_send, t_recv, (dp, dt), tile_peer(dt))
    for dp in range(n_pulse):
        for dt in range(1, half):
            slot = lax.rem(me_p + n_pulse - dp, n_pulse) * half + lax.rem(chip + half - dt, half)
            arrive(slot, t_send, t_recv, (dp, dt), tile_peer(dt))

    to_scalar = pltpu.make_async_copy(meta_ref.at[core], scal_ref, s_sem)
    to_scalar.start()
    meta_move = pltpu.make_async_remote_copy(
        src_ref=meta_ref.at[core], dst_ref=meta_ref.at[core],
        send_sem=p_send.at[2], recv_sem=p_recv.at[2],
        device_id=(me_p, partner), device_id_type=MESH,
    )
    meta_move.start()
    x = win_ref[...].astype(F32)
    r = lax.broadcasted_iota(jnp.int32, x.shape, 1)
    y = jnp.where(r < p_dev, -1.0, 1.0) * pltpu.roll(x, p_dev, 1)
    x_ref[0] = x.reshape(rows, win).astype(BF16)
    x_ref[1] = y.reshape(rows, win).astype(BF16)

    def compress(n, carry):
        load_filter(n).wait()
        acc = jnp.dot(x_ref[0], filt_buf[n, 0], preferred_element_type=F32) + jnp.dot(
            x_ref[1], filt_buf[n, 1], preferred_element_type=F32
        )
        acc = acc.astype(BF16).astype(F32)
        for c in range(chunk // LANES):
            prof_ref[pl.ds(n * (chunk // LANES) + c, rows, stride=stride), :] = acc[
                :, c * LANES : (c + 1) * LANES
            ]
        return carry

    lax.fori_loop(0, chunks, compress, 0)
    to_scalar.wait()
    lane8 = lax.broadcasted_iota(jnp.int32, (pieces, LANES), 1)

    def cut_bands(tile):
        def owner(d, carry):
            for p in range(p_dev):
                start = scal_ref[d, 0, 4 * rows8 + tile * p_dev + p]
                q = start >> 7
                r = start & (LANES - 1)
                turn = (LANES - r) & (LANES - 1)
                keep = lane8 < LANES - r
                for part in range(2):
                    row = d * rows8 + part * p_dev + p
                    low = pltpu.roll(prof_ref[pl.ds(row * stride + q, pieces), :], turn, 1)
                    high = pltpu.roll(prof_ref[pl.ds(row * stride + q + 1, pieces), :], turn, 1)
                    here = jnp.where(keep, low, high)
                    after = pltpu.roll(jnp.where(lane8 == 0, high, here), LANES - 1, 1)
                    cut_ref[pl.ds(row * pieces, pieces), :] = here
                    cut_ref[pl.ds((rows + row) * pieces, pieces), :] = after
            return carry

        lax.fori_loop(0, n_dev, owner, 0, unroll=4)

    cut_bands(partner)
    for c in range(pieces):
        for b in range(2):
            out_buf[b, :, c * LANES : (c + 1) * LANES] = cut_ref[
                pl.ds(b * rows * pieces + c, rows, stride=pieces), :
            ].astype(BF16)
    band_moves = [
        pltpu.make_async_remote_copy(
            src_ref=out_buf.at[b], dst_ref=bands_ref.at[b, core],
            send_sem=p_send.at[b], recv_sem=p_recv.at[b],
            device_id=(me_p, partner), device_id_type=MESH,
        )
        for b in range(2)
    ]
    for move in band_moves:
        move.start()
    cut_bands(me_t)
    for c in range(pieces):
        for b in range(2):
            bands_ref[b, core, :, c * LANES : (c + 1) * LANES] = cut_ref[
                pl.ds(b * rows * pieces + c, rows, stride=pieces), :
            ].astype(BF16)
    pltpu.make_async_remote_copy(
        src_ref=meta_ref.at[1 - core], dst_ref=meta_ref.at[1 - core],
        send_sem=p_send.at[2], recv_sem=p_recv.at[2],
        device_id=(me_p, partner), device_id_type=MESH,
    ).wait_recv()
    meta = meta_ref[...].reshape(2 * n_dev, meta_ref.shape[3]).astype(F32).astype(BF16)
    blk = spread(meta, 0, rows8, n_rows)
    fine = spread(meta, 1, rows8, n_rows) * (1.0 / 16.0)
    dop = spread(meta, 2, rows8, n_rows) + DOP_SPLIT * spread(meta, 3, rows8, n_rows)
    sel = lax.broadcasted_iota(jnp.int32, (2 * steps, n_rows), 0)
    col = lax.broadcasted_iota(jnp.int32, (2 * steps, n_rows), 1)
    in_block = (sel // 2).astype(F32) == blk
    same = in_block & (sel % 2 == (col % rows8) // p_dev)
    zero = jnp.zeros((2 * steps, n_rows), F32)
    p_left = jnp.concatenate([jnp.where(same, 1.0 - fine, zero), jnp.where(same, fine, zero)], 1)
    q_left = jnp.concatenate([jnp.where(same, -1.0, zero), jnp.where(same, 1.0, zero)], 1)
    left = jnp.concatenate([p_left, q_left], 0).astype(BF16)
    for b in range(2):
        pltpu.make_async_remote_copy(
            src_ref=out_buf.at[b], dst_ref=bands_ref.at[b, 1 - core],
            send_sem=p_send.at[b], recv_sem=p_recv.at[b],
            device_id=(me_p, partner), device_id_type=MESH,
        ).wait_recv()
    bands = bands_ref[...].reshape(2 * n_rows, band)
    pq = jnp.dot(left, bands, preferred_element_type=F32)
    k = 2 * steps
    x = 4.0 * pq[:k] + 1.5 * pq[k:]
    y = 1.5 * pq[:k] + 0.875 * pq[k:]
    xs = jnp.concatenate(thirds(x) + thirds(y), 0)
    d6 = lax.dot_general(xs, bands, (((1,), (1,)), ((), ())), preferred_element_type=F32)
    dx = d6[2 * k : 3 * k] + d6[k : 2 * k] + d6[:k]
    dy = d6[5 * k : 6 * k] + d6[4 * k : 5 * k] + d6[3 * k : 4 * k]
    h = ((1.0 - fine) * dx[:, :n_rows] - dy[:, :n_rows]) + (
        fine * dx[:, n_rows:] + dy[:, n_rows:]
    )
    hr = jnp.sum(jnp.where(in_block & (sel % 2 == 0), h, 0.0), axis=0, keepdims=True)
    hi = jnp.sum(jnp.where(in_block & (sel % 2 == 1), h, 0.0), axis=0, keepdims=True)
    both = jnp.concatenate([hr, hi, jnp.zeros((6, n_rows), F32)], 0)
    part1 = (lax.broadcasted_iota(jnp.int32, (8, n_rows), 1) % rows8) >= p_dev
    other = swap_parts(both, part1, p_dev)
    hr, hi, hr_o, hi_o = both[0:1], both[1:2], other[0:1], other[1:2]
    one = part1[0:1]
    g_ref[0:1] = jnp.where(one, hr_o + hi, hr + hi_o)
    g_ref[1:2] = jnp.where(one, hr - hi_o, hr_o - hi)
    g_moves = [
        pltpu.make_async_remote_copy(
            src_ref=g_ref, dst_ref=got_ref.at[d],
            send_sem=g_send.at[d], recv_sem=g_recv.at[d],
            device_id=any_tile(d), device_id_type=MESH,
        )
        for d in range(1, n_tile)
    ]
    for move in g_moves:
        move.start()
    total_rows = r_dev * n_pulse
    image_row = me_p * r_dev + lax.broadcasted_iota(jnp.int32, (r_dev, n_rows), 0)
    turns = dop.astype(jnp.int32) * image_row
    if total_rows & (total_rows - 1):
        turns = turns % total_rows
    else:
        turns = turns & (total_rows - 1)
    angle = 2.0 * jnp.pi * turns.astype(F32) / total_rows
    norm = 1.0 / jnp.sqrt(F32(n_rows // 2))
    er = (jnp.cos(angle) * norm).astype(BF16).astype(F32)
    ei = (jnp.sin(angle) * norm).astype(BF16).astype(F32)
    square = (n_rows, n_rows)
    diagonal = lax.broadcasted_iota(jnp.int32, square, 0) == lax.broadcasted_iota(jnp.int32, square, 1)
    fine_col = jnp.sum(jnp.where(diagonal, fine, 0.0), axis=1, keepdims=True)
    for s in range(pieces):
        cols = slice(s * LANES, (s + 1) * LANES)
        b0 = bands_ref[0, :, :, cols].reshape(n_rows, LANES).astype(F32)
        b1 = bands_ref[1, :, :, cols].reshape(n_rows, LANES).astype(F32)
        bend = fine_col * (b1 - b0)
        pair = jnp.concatenate([b0 + bend, b1 + bend], 1).astype(BF16)
        samp_ref[:, 4 * s * LANES : 4 * (s + 1) * LANES] = jnp.dot(
            pair, up_ref[...], preferred_element_type=F32
        ).astype(BF16)
    put_samples = pltpu.make_async_copy(samp_ref, samp_out, o_sem)
    put_samples.start()
    total = g_ref[...]
    for d in range(1, n_tile):
        g_moves[d - 1].wait_recv()
        total = total + got_ref[d]
    g_re, g_im = total[0:1], total[1:2]
    scale = jnp.sqrt(g_re * g_re + g_im * g_im + 1.0)
    c_re = g_re / scale
    c_im = -g_im / scale
    alpha = jnp.where(one, -c_im, c_re)
    beta = jnp.where(one, c_re, c_im)
    w = (er * alpha - ei * beta, er * beta + ei * alpha)
    for z in range(2):
        here = pl.ds(z * r_dev, r_dev)
        left_ref[here, :] = w[z].astype(BF16)
    put_samples.wait()
    for c in started + [meta_move] + band_moves + g_moves:
        c.wait_send()


def focus(n_pulse, n_tile, r_dev, band, range_off, fine, dop, order, idx, raw, filt):
    p_dev = raw.shape[1]
    win, ups = filt.shape[1:]
    half = n_tile // 2
    n_dev = n_pulse * half
    rows = n_dev * 2 * p_dev
    n_rows = 2 * rows
    fields = 8 * p_dev + idx.size
    width = fields + -fields % LANES
    chunk = 2 * LANES
    sem = pltpu.SemaphoreType.DMA
    return pl.pallas_call(
        functools.partial(focus_kernel, n_pulse, n_tile, r_dev),
        out_shape=(
            jax.ShapeDtypeStruct((2 * r_dev, n_rows), BF16),
            jax.ShapeDtypeStruct((n_rows, 4 * band), BF16),
        ),
        in_specs=[pl.BlockSpec(memory_space=pltpu.SMEM)] * 5
        + [pl.BlockSpec(memory_space=pltpu.VMEM), pl.BlockSpec(memory_space=pl.ANY)],
        out_specs=[pl.BlockSpec(memory_space=pltpu.VMEM), pl.BlockSpec(memory_space=pl.ANY)],
        scratch_shapes=[
            pltpu.VMEM((n_rows, 4 * band), BF16),
            sem,
            pltpu.VMEM((2, 2, rows, band), BF16),
            pltpu.VMEM((2 * LANES, 4 * LANES), BF16),
            pltpu.VMEM((n_dev, 2 * p_dev, win), BF16),
            pltpu.VMEM((2, n_dev, 1, width), jnp.int32),
            pltpu.SMEM((n_dev, 1, width), jnp.int32),
            pltpu.VMEM((ups // chunk, 2, win, chunk), BF16),
            pltpu.VMEM((2, rows, win), BF16),
            pltpu.VMEM((rows * (ups // LANES) + 8, LANES), F32),
            pltpu.VMEM((2 * rows * (band // LANES), LANES), F32),
            pltpu.VMEM((2, rows, band), BF16),
            pltpu.VMEM((2, n_rows), F32),
            pltpu.VMEM((n_tile, 2, n_rows), F32),
            sem((ups // chunk,)),
            sem,
            sem((2, n_pulse)),
            sem((2, n_pulse)),
            sem((2, n_pulse, half)),
            sem((2, n_pulse, half)),
            sem((3,)),
            sem((3,)),
            sem((n_tile,)),
            sem((n_tile,)),
        ],
        compiler_params=pltpu.CompilerParams(
            collective_id=0, has_side_effects=True, vmem_limit_bytes=VMEM_LIMIT
        ),
    )(range_off, fine, dop, order, idx, raw, filt)


def image_kernel(left_ref, samp_ref, out_ref):
    r_dev = out_ref.shape[1]
    res = jnp.dot(left_ref[...], samp_ref[...], preferred_element_type=F32).astype(BF16)
    for z in range(2):
        out_ref[z] = res[z * r_dev : (z + 1) * r_dev]


def image(left, samples, r_dev):
    k, cols = samples.shape
    width = cols // 4
    return pl.pallas_call(
        image_kernel,
        grid=(cols // width,),
        out_shape=jax.ShapeDtypeStruct((2, r_dev, cols), BF16),
        in_specs=[
            pl.BlockSpec(left.shape, lambda i: (0, 0)),
            pl.BlockSpec((k, width), lambda i: (0, i)),
        ],
        out_specs=pl.BlockSpec((2, r_dev, width), lambda i: (0, 0, i)),
        compiler_params=pltpu.CompilerParams(vmem_limit_bytes=VMEM_LIMIT),
    )(left, samples)


BAND = 1024
R_DEV = 128


def shards(raw, filt, range_off, fine, dop, pulse_order, band_idx):
    n_pulse = lax.axis_size("pulse")
    n_tile = lax.axis_size("tile")
    left, samples = focus(
        n_pulse, n_tile, R_DEV, BAND, range_off, fine, dop, pulse_order, band_idx.T, raw, filt
    )
    return image(left, samples, R_DEV)


def solution(mesh):
    return jax.shard_map(
        shards,
        mesh=mesh,
        in_specs=(
            P(None, ("pulse", "tile"), None),
            P(),
            P(("pulse", "tile")),
            P(("pulse", "tile")),
            P(("pulse", "tile")),
            P(("pulse", "tile"), None),
            P(None, ("pulse", "tile")),
        ),
        out_specs=P(None, "pulse", "tile"),
        check_vma=False,
    )
```

profile of v0, /device:TPU:0, one launch (start us, length us, event | category | flops | bytes accessed | tf_op | source)
XLA Modules:
  0.0 29.4 jit_solution(4920594640274798214)
XLA Ops:
  0.0 25.1 %shard_map.73 = (bf16[256,256]{1,0:T(8,128)(2,1)}, bf16[256,4096]{1,0:T(8,128)(2,1)}) custom-call(s32[4]{0:T(128)} %off_ref.1, s32[4]{0:T(128)} %fine_ref.1, s32[4]{0:T(128)} %dop_ref.1, s32[1,4]{1,0:T(1,128)} %order_ref.1, s32[4,8]{1,0:T(4,128)} %bitcast.1, bf16[2,4,2048]{2,1,0:T(4,128)(2,1)} %raw_ref.1, bf16[2,1024,2048]{2,1,0:T(8,128)(2,1)} %filt_ref.1), custom_call_target="tpu_custom_call" | custom-call | tf_op jit(solution)/shard_map/pallas_call | solution.py:331
  25.1 4.4 %shard_map.74 = bf16[2,128,4096]{2,1,0:T(8,128)(2,1)} custom-call(bf16[256,256]{1,0:T(8,128)(2,1)} %get-tuple-element.7.left_ref, bf16[256,4096]{1,0:T(8,128)(2,1)} %get-tuple-element.8.samp_ref), custom_call_target="tpu_custom_call" | custom-call | tf_op jit(solution)/shard_map/pallas_call | solution.py:382
where the time goes:
time: 29.7 us; the launch traced here: 29.4 us
  Pallas kernels  29.4 us (99%)
    pallas_call x1, Pallas kernels, focus(): pl.pallas_call(functools.partial(focus_kernel, n_pulse, n_tile, r_dev), o...  25.1 us
    pallas_call x1, Pallas kernels, image(): pl.pallas_call(image_kernel, grid=(cols // width,), out_shape=jax.ShapeDt...  4.35 us

commit v1 on v0

--- a/solution.py
+++ b/solution.py
@@ -12,7 +12,8 @@
 MESH = pl.DeviceIdType.MESH
 LANES = 128
 DOP_SPLIT = 32
-VMEM_LIMIT = 60 * 1024 * 1024
+VMEM_LIMIT = 44 * 1024 * 1024
+IMAGE_VMEM = 16 * 1024 * 1024
 
 
 def spread(meta, field, rows8, n_rows):
@@ -39,10 +40,11 @@
 
 def focus_kernel(
     n_pulse, n_tile, r_dev,
-    off_ref, fine_ref, dop_ref, order_ref, idx_ref, raw_ref, filt_ref,
-    left_ref, samp_out,
-    samp_ref, o_sem, bands_ref, up_ref, win_ref, meta_ref, scal_ref, filt_buf, x_ref, prof_ref, cut_ref, out_buf, g_ref, got_ref,
-    f_sem, s_sem, z_send, z_recv, t_send, t_recv, p_send, p_recv, g_send, g_recv,
+    off_in, fine_in, dop_in, order_in, idx_in, raw_in, filt_ref,
+    left_ref, samp_ref,
+    off_ref, fine_ref, dop_ref, order_ref, idx_ref, raw_ref,
+    bands_ref, up_ref, win_ref, meta_ref, scal_ref, filt_buf, x_ref, prof_ref, cut_ref, out_buf, g_ref, got_ref,
+    i_sem, f_sem, s_sem, z_send, z_recv, t_send, t_recv, p_send, p_recv, g_send, g_recv,
 ):
     me_p = lax.axis_index("pulse")
     me_t = lax.axis_index("tile")
@@ -60,14 +62,27 @@
     n_rows = 2 * rows
     chunks, chunk = filt_buf.shape[0], filt_buf.shape[3]
     stride = prof_ref.shape[0] // rows
-    band = bands_ref.shape[3]
+    ext = bands_ref.shape[2]
+    band = ext - LANES
     pieces = band // LANES
+
+    def pulse_at(i):
+        low, high = me_p, n_pulse - 1 - me_p
+        both = jnp.minimum(low, high)
+        two_sided = i <= 2 * both
+        dist = jnp.where(two_sided, (i + 1) // 2, i - both)
+        up = jnp.where(two_sided, i % 2, jnp.where(high > low, 1, 0))
+        return me_p + (2 * up - 1) * dist
 
     def pulse_peer(d):
         return (lax.rem(me_p + d, n_pulse), me_t)
 
-    def tile_peer(d):
-        return (me_p, lax.rem(chip + d, half) * 2 + core)
+    def flip(k):
+        bits = [1 << n for n in range(half.bit_length() - 1)]
+        return sum(((chip // b + k // b) % 2) * b for b in bits)
+
+    def tile_peer(k):
+        return (me_p, flip(k) * 2 + core)
 
     def any_tile(d):
         return (me_p, lax.rem(me_t + d, n_tile))
@@ -83,8 +98,19 @@
             filt_ref.at[:, :, pl.ds(n * chunk, chunk)], filt_buf.at[n], f_sem.at[n]
         )
 
+    inputs = [
+        pltpu.make_async_copy(src, dst, i_sem.at[n])
+        for n, (src, dst) in enumerate(
+            [(raw_in, raw_ref), (off_in, off_ref), (order_in, order_ref)]
+            + [(fine_in, fine_ref), (dop_in, dop_ref), (idx_in, idx_ref)]
+        )
+    ]
+    for copy in inputs:
+        copy.start()
     for n in range(chunks):
         load_filter(n).start()
+    for copy in inputs:
+        copy.wait()
 
     raw = jnp.concatenate([raw_ref[0].astype(F32), raw_ref[1].astype(F32)], 0)
     row = lax.broadcasted_iota(jnp.int32, (rows8, win), 0)
@@ -134,18 +160,21 @@
         for c in copies(*args):
             c.wait_recv()
 
-    for d in reversed(range(1, n_pulse)):
-        send(mine, z_send, z_recv, (d,), pulse_peer(d))
-    for dp in range(n_pulse):
-        slot = lax.rem(me_p + n_pulse - dp, n_pulse) * half + chip
-        if dp:
-            arrive(slot, z_send, z_recv, (dp,), pulse_peer(dp))
-        for dt in reversed(range(1, half)):
-            send(slot, t_send, t_recv, (dp, dt), tile_peer(dt))
-    for dp in range(n_pulse):
-        for dt in range(1, half):
-            slot = lax.rem(me_p + n_pulse - dp, n_pulse) * half + lax.rem(chip + half - dt, half)
-            arrive(slot, t_send, t_recv, (dp, dt), tile_peer(dt))
+    nearest = [pulse_at(i) for i in range(1, n_pulse)]
+    for q in reversed(nearest):
+        d = lax.rem(q - me_p + n_pulse, n_pulse)
+        send(mine, z_send, z_recv, (d,), (q, me_t))
+    for q in [me_p] + nearest:
+        dp = lax.rem(me_p - q + n_pulse, n_pulse)
+        slot = q * half + chip
+        if q is not me_p:
+            arrive(slot, z_send, z_recv, (dp,), (q, me_t))
+        for k in reversed(range(1, half)):
+            send(slot, t_send, t_recv, (dp, k), tile_peer(k))
+    for q in [me_p] + nearest:
+        dp = lax.rem(me_p - q + n_pulse, n_pulse)
+        for k in range(1, half):
+            arrive(q * half + flip(k), t_send, t_recv, (dp, k), tile_peer(k))
 
     to_scalar = pltpu.make_async_copy(meta_ref.at[core], scal_ref, s_sem)
     to_scalar.start()
@@ -155,29 +184,26 @@
         device_id=(me_p, partner), device_id_type=MESH,
     )
     meta_move.start()
+    for n in range(chunks):
+        load_filter(n).wait()
     x = win_ref[...].astype(F32)
     r = lax.broadcasted_iota(jnp.int32, x.shape, 1)
     y = jnp.where(r < p_dev, -1.0, 1.0) * pltpu.roll(x, p_dev, 1)
     x_ref[0] = x.reshape(rows, win).astype(BF16)
     x_ref[1] = y.reshape(rows, win).astype(BF16)
 
-    def compress(n, carry):
-        load_filter(n).wait()
+    for n in range(chunks):
         acc = jnp.dot(x_ref[0], filt_buf[n, 0], preferred_element_type=F32) + jnp.dot(
             x_ref[1], filt_buf[n, 1], preferred_element_type=F32
         )
-        acc = acc.astype(BF16).astype(F32)
         for c in range(chunk // LANES):
             prof_ref[pl.ds(n * (chunk // LANES) + c, rows, stride=stride), :] = acc[
                 :, c * LANES : (c + 1) * LANES
             ]
-        return carry
-
-    lax.fori_loop(0, chunks, compress, 0)
     to_scalar.wait()
     lane8 = lax.broadcasted_iota(jnp.int32, (pieces, LANES), 1)
 
-    def cut_bands(tile):
+    def cut_bands(tile, part_of):
         def owner(d, carry):
             for p in range(p_dev):
                 start = scal_ref[d, 0, 4 * rows8 + tile * p_dev + p]
@@ -189,36 +215,38 @@
                     row = d * rows8 + part * p_dev + p
                     low = pltpu.roll(prof_ref[pl.ds(row * stride + q, pieces), :], turn, 1)
                     high = pltpu.roll(prof_ref[pl.ds(row * stride + q + 1, pieces), :], turn, 1)
-                    here = jnp.where(keep, low, high)
-                    after = pltpu.roll(jnp.where(lane8 == 0, high, here), LANES - 1, 1)
-                    cut_ref[pl.ds(row * pieces, pieces), :] = here
-                    cut_ref[pl.ds((rows + row) * pieces, pieces), :] = after
+                    at = row * (pieces + 1)
+                    cut_ref[pl.ds(at + 1, pieces), :] = high
+                    cut_ref[pl.ds(at, pieces), :] = jnp.where(keep, low, high)
             return carry
 
-        lax.fori_loop(0, n_dev, owner, 0, unroll=4)
-
-    cut_bands(partner)
-    for c in range(pieces):
-        for b in range(2):
-            out_buf[b, :, c * LANES : (c + 1) * LANES] = cut_ref[
-                pl.ds(b * rows * pieces + c, rows, stride=pieces), :
-            ].astype(BF16)
-    band_moves = [
-        pltpu.make_async_remote_copy(
-            src_ref=out_buf.at[b], dst_ref=bands_ref.at[b, core],
-            send_sem=p_send.at[b], recv_sem=p_recv.at[b],
+        n = n_dev // 2
+        lax.fori_loop(part_of * n, (part_of + 1) * n, owner, 0, unroll=4)
+
+    def pack(c, part_of):
+        first = part_of * (rows // 2) * (pieces + 1) + c
+        return cut_ref[pl.ds(first, rows // 2, stride=pieces + 1), :].astype(BF16)
+
+    def band_move(part_of, to):
+        here = pl.ds(part_of * (rows // 2), rows // 2)
+        return pltpu.make_async_remote_copy(
+            src_ref=out_buf.at[here], dst_ref=bands_ref.at[to, here],
+            send_sem=p_send.at[part_of], recv_sem=p_recv.at[part_of],
             device_id=(me_p, partner), device_id_type=MESH,
         )
-        for b in range(2)
-    ]
-    for move in band_moves:
-        move.start()
-    cut_bands(me_t)
-    for c in range(pieces):
-        for b in range(2):
-            bands_ref[b, core, :, c * LANES : (c + 1) * LANES] = cut_ref[
-                pl.ds(b * rows * pieces + c, rows, stride=pieces), :
-            ].astype(BF16)
+
+    band_moves = [band_move(part_of, core) for part_of in range(2)]
+    for part_of in range(2):
+        cut_bands(partner, part_of)
+        here = slice(part_of * (rows // 2), (part_of + 1) * (rows // 2))
+        for c in range(pieces + 1):
+            out_buf[here, c * LANES : (c + 1) * LANES] = pack(c, part_of)
+        band_moves[part_of].start()
+    for part_of in range(2):
+        cut_bands(me_t, part_of)
+        here = slice(part_of * (rows // 2), (part_of + 1) * (rows // 2))
+        for c in range(pieces + 1):
+            bands_ref[core, here, c * LANES : (c + 1) * LANES] = pack(c, part_of)
     pltpu.make_async_remote_copy(
         src_ref=meta_ref.at[1 - core], dst_ref=meta_ref.at[1 - core],
         send_sem=p_send.at[2], recv_sem=p_recv.at[2],
@@ -233,27 +261,25 @@
     in_block = (sel // 2).astype(F32) == blk
     same = in_block & (sel % 2 == (col % rows8) // p_dev)
     zero = jnp.zeros((2 * steps, n_rows), F32)
-    p_left = jnp.concatenate([jnp.where(same, 1.0 - fine, zero), jnp.where(same, fine, zero)], 1)
-    q_left = jnp.concatenate([jnp.where(same, -1.0, zero), jnp.where(same, 1.0, zero)], 1)
-    left = jnp.concatenate([p_left, q_left], 0).astype(BF16)
-    for b in range(2):
-        pltpu.make_async_remote_copy(
-            src_ref=out_buf.at[b], dst_ref=bands_ref.at[b, 1 - core],
-            send_sem=p_send.at[b], recv_sem=p_recv.at[b],
-            device_id=(me_p, partner), device_id_type=MESH,
-        ).wait_recv()
-    bands = bands_ref[...].reshape(2 * n_rows, band)
-    pq = jnp.dot(left, bands, preferred_element_type=F32)
+    left = jnp.concatenate([jnp.where(same, 1.0, zero), jnp.where(same, fine, zero)], 0).astype(BF16)
+    for part_of in range(2):
+        band_move(part_of, 1 - core).wait_recv()
+    bands = bands_ref[...].reshape(n_rows, ext)
+    ab = jnp.dot(left, bands, preferred_element_type=F32)
     k = 2 * steps
-    x = 4.0 * pq[:k] + 1.5 * pq[k:]
-    y = 1.5 * pq[:k] + 0.875 * pq[k:]
-    xs = jnp.concatenate(thirds(x) + thirds(y), 0)
+    a, b = ab[:k], ab[k:]
+    pc = a - b + pltpu.roll(b, ext - 1, 1)
+    qc = pltpu.roll(a, ext - 1, 1) - a
+    inside = lax.broadcasted_iota(jnp.int32, pc.shape, 1) < band
+    x = jnp.where(inside, 4.0 * pc + 1.5 * qc, 0.0)
+    y = jnp.where(inside, 1.5 * pc + 0.875 * qc, 0.0)
+    x0 = x - y + pltpu.roll(y, 1, 1)
+    x1 = pltpu.roll(x, 1, 1) - x
+    xs = jnp.concatenate(thirds(x0) + thirds(x1), 0)
     d6 = lax.dot_general(xs, bands, (((1,), (1,)), ((), ())), preferred_element_type=F32)
-    dx = d6[2 * k : 3 * k] + d6[k : 2 * k] + d6[:k]
-    dy = d6[5 * k : 6 * k] + d6[4 * k : 5 * k] + d6[3 * k : 4 * k]
-    h = ((1.0 - fine) * dx[:, :n_rows] - dy[:, :n_rows]) + (
-        fine * dx[:, n_rows:] + dy[:, n_rows:]
-    )
+    d0 = d6[2 * k : 3 * k] + d6[k : 2 * k] + d6[:k]
+    d1 = d6[5 * k : 6 * k] + d6[4 * k : 5 * k] + d6[3 * k : 4 * k]
+    h = d0 + fine * d1
     hr = jnp.sum(jnp.where(in_block & (sel % 2 == 0), h, 0.0), axis=0, keepdims=True)
     hi = jnp.sum(jnp.where(in_block & (sel % 2 == 1), h, 0.0), axis=0, keepdims=True)
     both = jnp.concatenate([hr, hi, jnp.zeros((6, n_rows), F32)], 0)
@@ -287,17 +313,16 @@
     square = (n_rows, n_rows)
     diagonal = lax.broadcasted_iota(jnp.int32, square, 0) == lax.broadcasted_iota(jnp.int32, square, 1)
     fine_col = jnp.sum(jnp.where(diagonal, fine, 0.0), axis=1, keepdims=True)
+    lane = lax.broadcasted_iota(jnp.int32, (n_rows, LANES), 1)
     for s in range(pieces):
-        cols = slice(s * LANES, (s + 1) * LANES)
-        b0 = bands_ref[0, :, :, cols].reshape(n_rows, LANES).astype(F32)
-        b1 = bands_ref[1, :, :, cols].reshape(n_rows, LANES).astype(F32)
+        b0 = bands_ref[:, :, s * LANES : (s + 1) * LANES].reshape(n_rows, LANES).astype(F32)
+        b1 = bands_ref[:, :, (s + 1) * LANES : (s + 2) * LANES].reshape(n_rows, LANES).astype(F32)
+        b1 = pltpu.roll(jnp.where(lane == 0, b1, b0), LANES - 1, 1)
         bend = fine_col * (b1 - b0)
         pair = jnp.concatenate([b0 + bend, b1 + bend], 1).astype(BF16)
         samp_ref[:, 4 * s * LANES : 4 * (s + 1) * LANES] = jnp.dot(
             pair, up_ref[...], preferred_element_type=F32
         ).astype(BF16)
-    put_samples = pltpu.make_async_copy(samp_ref, samp_out, o_sem)
-    put_samples.start()
     total = g_ref[...]
     for d in range(1, n_tile):
         g_moves[d - 1].wait_recv()
@@ -312,7 +337,6 @@
     for z in range(2):
         here = pl.ds(z * r_dev, r_dev)
         left_ref[here, :] = w[z].astype(BF16)
-    put_samples.wait()
     for c in started + [meta_move] + band_moves + g_moves:
         c.wait_send()
 
@@ -331,16 +355,15 @@
     return pl.pallas_call(
         functools.partial(focus_kernel, n_pulse, n_tile, r_dev),
         out_shape=(
-            jax.ShapeDtypeStruct((2 * r_dev, n_rows), BF16),
-            jax.ShapeDtypeStruct((n_rows, 4 * band), BF16),
+            pltpu.VMEM((2 * r_dev, n_rows), BF16),
+            pltpu.VMEM((n_rows, 4 * band), BF16),
         ),
-        in_specs=[pl.BlockSpec(memory_space=pltpu.SMEM)] * 5
-        + [pl.BlockSpec(memory_space=pltpu.VMEM), pl.BlockSpec(memory_space=pl.ANY)],
-        out_specs=[pl.BlockSpec(memory_space=pltpu.VMEM), pl.BlockSpec(memory_space=pl.ANY)],
+        in_specs=[pl.BlockSpec(memory_space=pltpu.HBM)] * 7,
+        out_specs=[pl.BlockSpec(memory_space=pltpu.VMEM)] * 2,
         scratch_shapes=[
-            pltpu.VMEM((n_rows, 4 * band), BF16),
-            sem,
-            pltpu.VMEM((2, 2, rows, band), BF16),
+            *[pltpu.SMEM(a.shape, jnp.int32) for a in (range_off, fine, dop, order, idx)],
+            pltpu.VMEM(raw.shape, BF16),
+            pltpu.VMEM((2, rows, band + LANES), BF16),
             pltpu.VMEM((2 * LANES, 4 * LANES), BF16),
             pltpu.VMEM((n_dev, 2 * p_dev, win), BF16),
             pltpu.VMEM((2, n_dev, 1, width), jnp.int32),
@@ -348,10 +371,11 @@
             pltpu.VMEM((ups // chunk, 2, win, chunk), BF16),
             pltpu.VMEM((2, rows, win), BF16),
             pltpu.VMEM((rows * (ups // LANES) + 8, LANES), F32),
-            pltpu.VMEM((2 * rows * (band // LANES), LANES), F32),
-            pltpu.VMEM((2, rows, band), BF16),
+            pltpu.VMEM((rows * (band // LANES + 1), LANES), F32),
+            pltpu.VMEM((rows, band + LANES), BF16),
             pltpu.VMEM((2, n_rows), F32),
             pltpu.VMEM((n_tile, 2, n_rows), F32),
+            sem((6,)),
             sem((ups // chunk,)),
             sem,
             sem((2, n_pulse)),
@@ -366,29 +390,35 @@
         compiler_params=pltpu.CompilerParams(
             collective_id=0, has_side_effects=True, vmem_limit_bytes=VMEM_LIMIT
         ),
-    )(range_off, fine, dop, order, idx, raw, filt)
-
-
-def image_kernel(left_ref, samp_ref, out_ref):
+    )(*[pltpu.with_memory_space_constraint(a, pltpu.HBM) for a in (range_off, fine, dop, order, idx, raw, filt)])
+
+
+def image_kernel(left_ref, samp_ref, out_ref, res_ref, sem):
     r_dev = out_ref.shape[1]
-    res = jnp.dot(left_ref[...], samp_ref[...], preferred_element_type=F32).astype(BF16)
-    for z in range(2):
-        out_ref[z] = res[z * r_dev : (z + 1) * r_dev]
+    parts = sem.shape[0]
+    width = out_ref.shape[2] // parts
+    moves = []
+    for i in range(parts):
+        cols = pl.ds(i * width, width)
+        res = jnp.dot(left_ref[...], samp_ref[:, cols], preferred_element_type=F32).astype(BF16)
+        for z in range(2):
+            res_ref[z, :, cols] = res[z * r_dev : (z + 1) * r_dev]
+        move = pltpu.make_async_copy(res_ref.at[:, :, cols], out_ref.at[:, :, cols], sem.at[i])
+        move.start()
+        moves.append(move)
+    for move in moves:
+        move.wait()
 
 
 def image(left, samples, r_dev):
-    k, cols = samples.shape
-    width = cols // 4
+    cols = samples.shape[1]
     return pl.pallas_call(
         image_kernel,
-        grid=(cols // width,),
         out_shape=jax.ShapeDtypeStruct((2, r_dev, cols), BF16),
-        in_specs=[
-            pl.BlockSpec(left.shape, lambda i: (0, 0)),
-            pl.BlockSpec((k, width), lambda i: (0, i)),
-        ],
-        out_specs=pl.BlockSpec((2, r_dev, width), lambda i: (0, 0, i)),
-        compiler_params=pltpu.CompilerParams(vmem_limit_bytes=VMEM_LIMIT),
+        in_specs=[pl.BlockSpec(memory_space=pltpu.VMEM)] * 2,
+        out_specs=pl.BlockSpec(memory_space=pltpu.HBM),
+        scratch_shapes=[pltpu.VMEM((2, r_dev, cols), BF16), pltpu.SemaphoreType.DMA((8,))],
+        compiler_params=pltpu.CompilerParams(vmem_limit_bytes=IMAGE_VMEM),
     )(left, samples)
 
 

time: 29.7 us -> 22.3 us (0.75)
  Pallas kernels: 29.4 us -> 22.1 us
    pallas_call x1, Pallas kernels: 25.1 us -> 20.5 us  [focus(): pl.pallas_call(functools.partial(focus_kernel, n_pulse, n_tile, r_dev), o...]
    pallas_call x1, Pallas kernels: 4.35 us -> 1.61 us  [image(): pl.pallas_call(image_kernel, out_shape=jax.ShapeDtypeStruct((2, r_dev, co...]
where the time goes in v1:
time: 22.3 us; the launch traced here: 22.1 us
  Pallas kernels  22.1 us (99%)
    pallas_call x1, Pallas kernels, focus(): pl.pallas_call(functools.partial(focus_kernel, n_pulse, n_tile, r_dev), o...  20.5 us
    pallas_call x1, Pallas kernels, image(): pl.pallas_call(image_kernel, out_shape=jax.ShapeDtypeStruct((2, r_dev, co...  1.61 us

profile of v1, /device:TPU:0, one launch (start us, length us, event | category | flops | bytes accessed | tf_op | source)
XLA Modules:
  0.0 22.1 jit_solution(17464647142611245035)
XLA Ops:
  0.0 20.5 %shard_map.73 = (bf16[256,256]{1,0:T(8,128)(2,1)S(1)}, bf16[256,4096]{1,0:T(8,128)(2,1)S(1)}) custom-call(s32[4]{0:T(128)} %off_in.1, s32[4]{0:T(128)} %fine_in.1, s32[4]{0:T(128)} %dop_in.1, s32[1,4]{1,0:T(1,128)} %order_in.1, s32[4,8]{1,0:T(4,128)} %bitcast.1, bf16[2,4,2048]{2,1,0:T(4,128)(2,1)} %raw_in.1, bf16[2,1024,2048]{2,1,0:T(8,128)(2,1)} %filt_ref.1), custom_call_target="tpu_custom_call" | custom-call | tf_op jit(solution)/shard_map/pallas_call | solution.py:355
  20.5 1.6 %shard_map.74 = bf16[2,128,4096]{2,1,0:T(8,128)(2,1)} custom-call(bf16[256,256]{1,0:T(8,128)(2,1)S(1)} %get-tuple-element.7.left_ref, bf16[256,4096]{1,0:T(8,128)(2,1)S(1)} %get-tuple-element.8.samp_ref), custom_call_target="tpu_custom_call" | custom-call | tf_op jit(solution)/shard_map/pallas_call | solution.py:415

commit v2 on v1

--- a/solution.py
+++ b/solution.py
@@ -44,7 +44,7 @@
     left_ref, samp_ref,
     off_ref, fine_ref, dop_ref, order_ref, idx_ref, raw_ref,
     bands_ref, up_ref, win_ref, meta_ref, scal_ref, filt_buf, x_ref, prof_ref, cut_ref, out_buf, g_ref, got_ref,
-    i_sem, f_sem, s_sem, z_send, z_recv, t_send, t_recv, p_send, p_recv, g_send, g_recv,
+    past_sem, i_sem, f_sem, s_sem, z_send, z_recv, t_send, t_recv, p_send, p_recv, g_send, g_recv,
 ):
     me_p = lax.axis_index("pulse")
     me_t = lax.axis_index("tile")
@@ -90,8 +90,12 @@
     barrier = pltpu.get_barrier_semaphore()
     for d in range(1, n_pulse):
         pl.semaphore_signal(barrier, 1, device_id=pulse_peer(d), device_id_type=MESH)
-    for d in range(1, n_tile):
-        pl.semaphore_signal(barrier, 1, device_id=any_tile(d), device_id_type=MESH)
+    near = [1, 2] if half == 4 else list(range(1, half))
+    greeted = [tile_peer(k) for k in near] + [(me_p, partner)]
+    if half != 4:
+        greeted += [(me_p, flip(k) * 2 + 1 - core) for k in near]
+    for peer in greeted:
+        pl.semaphore_signal(barrier, 1, device_id=peer, device_id_type=MESH)
 
     def load_filter(n):
         return pltpu.make_async_copy(
@@ -107,10 +111,10 @@
     ]
     for copy in inputs:
         copy.start()
+    for copy in inputs:
+        copy.wait()
     for n in range(chunks):
         load_filter(n).start()
-    for copy in inputs:
-        copy.wait()
 
     raw = jnp.concatenate([raw_ref[0].astype(F32), raw_ref[1].astype(F32)], 0)
     row = lax.broadcasted_iota(jnp.int32, (rows8, win), 0)
@@ -138,7 +142,9 @@
     w = (c % 4).astype(F32) * 0.25
     up = jnp.where(j < LANES, 1.0 - w, w)
     up_ref[...] = jnp.where(j % LANES == c // 4, up, 0.0).astype(BF16)
-    pl.semaphore_wait(barrier, n_pulse - 1 + n_tile - 1)
+    pl.semaphore_wait(barrier, n_pulse - 1 + len(greeted))
+    if half == 4:
+        pl.semaphore_signal(past_sem, 1, device_id=tile_peer(1), device_id_type=MESH)
 
     def copies(slot, send, recv, at, target):
         return [
@@ -169,8 +175,14 @@
         slot = q * half + chip
         if q is not me_p:
             arrive(slot, z_send, z_recv, (dp,), (q, me_t))
+        else:
+            for k in near:
+                send(slot, t_send, t_recv, (dp, k), tile_peer(k))
+            if half == 4:
+                pl.semaphore_wait(past_sem, 1)
         for k in reversed(range(1, half)):
-            send(slot, t_send, t_recv, (dp, k), tile_peer(k))
+            if q is not me_p or k not in near:
+                send(slot, t_send, t_recv, (dp, k), tile_peer(k))
     for q in [me_p] + nearest:
         dp = lax.rem(me_p - q + n_pulse, n_pulse)
         for k in range(1, half):
@@ -375,6 +387,7 @@
             pltpu.VMEM((rows, band + LANES), BF16),
             pltpu.VMEM((2, n_rows), F32),
             pltpu.VMEM((n_tile, 2, n_rows), F32),
+            pltpu.SemaphoreType.REGULAR,
             sem((6,)),
             sem((ups // chunk,)),
             sem,

time: 22.3 us -> 21.7 us (0.973)
  Pallas kernels: 22.1 us -> 21.5 us
    pallas_call x1, Pallas kernels: 20.5 us -> 19.9 us  [focus(): pl.pallas_call(functools.partial(focus_kernel, n_pulse, n_tile, r_dev), o...]
where the time goes in v2:
time: 21.7 us; the launch traced here: 21.5 us
  Pallas kernels  21.5 us (99%)
    pallas_call x1, Pallas kernels, focus(): pl.pallas_call(functools.partial(focus_kernel, n_pulse, n_tile, r_dev), o...  19.9 us
    pallas_call x1, Pallas kernels, image(): pl.pallas_call(image_kernel, out_shape=jax.ShapeDtypeStruct((2, r_dev, co...  1.61 us

profile of v2, /device:TPU:0, one launch (start us, length us, event | category | flops | bytes accessed | tf_op | source)
XLA Modules:
  0.0 21.5 jit_solution(5669276883778244830)
XLA Ops:
  0.0 19.9 %shard_map.73 = (bf16[256,256]{1,0:T(8,128)(2,1)S(1)}, bf16[256,4096]{1,0:T(8,128)(2,1)S(1)}) custom-call(s32[4]{0:T(128)} %off_in.1, s32[4]{0:T(128)} %fine_in.1, s32[4]{0:T(128)} %dop_in.1, s32[1,4]{1,0:T(1,128)} %order_in.1, s32[4,8]{1,0:T(4,128)} %bitcast.1, bf16[2,4,2048]{2,1,0:T(4,128)(2,1)} %raw_in.1, bf16[2,1024,2048]{2,1,0:T(8,128)(2,1)} %filt_ref.1), custom_call_target="tpu_custom_call" | custom-call | tf_op jit(solution)/shard_map/pallas_call | solution.py:367
  19.9 1.6 %shard_map.74 = bf16[2,128,4096]{2,1,0:T(8,128)(2,1)} custom-call(bf16[256,256]{1,0:T(8,128)(2,1)S(1)} %get-tuple-element.7.left_ref, bf16[256,4096]{1,0:T(8,128)(2,1)S(1)} %get-tuple-element.8.samp_ref), custom_call_target="tpu_custom_call" | custom-call | tf_op jit(solution)/shard_map/pallas_call | solution.py:428

commit v3 on v2

--- a/solution.py
+++ b/solution.py
@@ -44,7 +44,7 @@
     left_ref, samp_ref,
     off_ref, fine_ref, dop_ref, order_ref, idx_ref, raw_ref,
     bands_ref, up_ref, win_ref, meta_ref, scal_ref, filt_buf, x_ref, prof_ref, cut_ref, out_buf, g_ref, got_ref,
-    past_sem, i_sem, f_sem, s_sem, z_send, z_recv, t_send, t_recv, p_send, p_recv, g_send, g_recv,
+    past_sem, i_sem, f_sem, s_sem, w_send, z_recv, t_recv, p_send, p_recv, g_send, g_recv,
 ):
     me_p = lax.axis_index("pulse")
     me_t = lax.axis_index("tile")
@@ -60,7 +60,8 @@
     rows8 = 2 * p_dev
     n_dev = n_pulse * half
     n_rows = 2 * rows
-    chunks, chunk = filt_buf.shape[0], filt_buf.shape[3]
+    chunk = 2 * LANES
+    chunks = filt_buf.shape[2] // chunk
     stride = prof_ref.shape[0] // rows
     ext = bands_ref.shape[2]
     band = ext - LANES
@@ -97,11 +98,7 @@
     for peer in greeted:
         pl.semaphore_signal(barrier, 1, device_id=peer, device_id_type=MESH)
 
-    def load_filter(n):
-        return pltpu.make_async_copy(
-            filt_ref.at[:, :, pl.ds(n * chunk, chunk)], filt_buf.at[n], f_sem.at[n]
-        )
-
+    load_filter = pltpu.make_async_copy(filt_ref, filt_buf, f_sem)
     inputs = [
         pltpu.make_async_copy(src, dst, i_sem.at[n])
         for n, (src, dst) in enumerate(
@@ -113,8 +110,7 @@
         copy.start()
     for copy in inputs:
         copy.wait()
-    for n in range(chunks):
-        load_filter(n).start()
+    load_filter.start()
 
     raw = jnp.concatenate([raw_ref[0].astype(F32), raw_ref[1].astype(F32)], 0)
     row = lax.broadcasted_iota(jnp.int32, (rows8, win), 0)
@@ -146,21 +142,18 @@
     if half == 4:
         pl.semaphore_signal(past_sem, 1, device_id=tile_peer(1), device_id_type=MESH)
 
-    def copies(slot, send, recv, at, target):
+    def copies(slot, recv, at, target):
         return [
             pltpu.make_async_remote_copy(
-                src_ref=ref, dst_ref=ref, send_sem=send.at[(a,) + at], recv_sem=recv.at[(a,) + at],
+                src_ref=ref, dst_ref=ref, send_sem=w_send.at[a], recv_sem=recv.at[(a,) + at],
                 device_id=target, device_id_type=MESH,
             )
             for a, ref in enumerate((win_ref.at[slot], meta_ref.at[core, slot]))
         ]
 
-    started = []
-
     def send(*args):
         for c in copies(*args):
             c.start()
-            started.append(c)
 
     def arrive(*args):
         for c in copies(*args):
@@ -169,24 +162,21 @@
     nearest = [pulse_at(i) for i in range(1, n_pulse)]
     for q in reversed(nearest):
         d = lax.rem(q - me_p + n_pulse, n_pulse)
-        send(mine, z_send, z_recv, (d,), (q, me_t))
+        send(mine, z_recv, (d,), (q, me_t))
     for q in [me_p] + nearest:
         dp = lax.rem(me_p - q + n_pulse, n_pulse)
         slot = q * half + chip
         if q is not me_p:
-            arrive(slot, z_send, z_recv, (dp,), (q, me_t))
+            arrive(slot, z_recv, (dp,), (q, me_t))
         else:
             for k in near:
-                send(slot, t_send, t_recv, (dp, k), tile_peer(k))
+                send(slot, t_recv, (), tile_peer(k))
             if half == 4:
                 pl.semaphore_wait(past_sem, 1)
         for k in reversed(range(1, half)):
             if q is not me_p or k not in near:
-                send(slot, t_send, t_recv, (dp, k), tile_peer(k))
-    for q in [me_p] + nearest:
-        dp = lax.rem(me_p - q + n_pulse, n_pulse)
-        for k in range(1, half):
-            arrive(q * half + flip(k), t_send, t_recv, (dp, k), tile_peer(k))
+                send(slot, t_recv, (), tile_peer(k))
+    arrive(pl.ds(0, n_pulse * (half - 1)), t_recv, (), tile_peer(1))
 
     to_scalar = pltpu.make_async_copy(meta_ref.at[core], scal_ref, s_sem)
     to_scalar.start()
@@ -196,8 +186,7 @@
         device_id=(me_p, partner), device_id_type=MESH,
     )
     meta_move.start()
-    for n in range(chunks):
-        load_filter(n).wait()
+    load_filter.wait()
     x = win_ref[...].astype(F32)
     r = lax.broadcasted_iota(jnp.int32, x.shape, 1)
     y = jnp.where(r < p_dev, -1.0, 1.0) * pltpu.roll(x, p_dev, 1)
@@ -205,8 +194,9 @@
     x_ref[1] = y.reshape(rows, win).astype(BF16)
 
     for n in range(chunks):
-        acc = jnp.dot(x_ref[0], filt_buf[n, 0], preferred_element_type=F32) + jnp.dot(
-            x_ref[1], filt_buf[n, 1], preferred_element_type=F32
+        cols = slice(n * chunk, (n + 1) * chunk)
+        acc = jnp.dot(x_ref[0], filt_buf[0, :, cols], preferred_element_type=F32) + jnp.dot(
+            x_ref[1], filt_buf[1, :, cols], preferred_element_type=F32
         )
         for c in range(chunk // LANES):
             prof_ref[pl.ds(n * (chunk // LANES) + c, rows, stride=stride), :] = acc[
@@ -304,7 +294,7 @@
     g_moves = [
         pltpu.make_async_remote_copy(
             src_ref=g_ref, dst_ref=got_ref.at[d],
-            send_sem=g_send.at[d], recv_sem=g_recv.at[d],
+            send_sem=g_send, recv_sem=g_recv,
             device_id=any_tile(d), device_id_type=MESH,
         )
         for d in range(1, n_tile)
@@ -336,8 +326,13 @@
             pair, up_ref[...], preferred_element_type=F32
         ).astype(BF16)
     total = g_ref[...]
+    got_all = got_ref.at[pl.ds(1, n_tile - 1)]
+    g_all = pltpu.make_async_remote_copy(
+        src_ref=got_all, dst_ref=got_all, send_sem=g_send, recv_sem=g_recv,
+        device_id=any_tile(1), device_id_type=MESH,
+    )
+    g_all.wait_recv()
     for d in range(1, n_tile):
-        g_moves[d - 1].wait_recv()
         total = total + got_ref[d]
     g_re, g_im = total[0:1], total[1:2]
     scale = jnp.sqrt(g_re * g_re + g_im * g_im + 1.0)
@@ -349,7 +344,7 @@
     for z in range(2):
         here = pl.ds(z * r_dev, r_dev)
         left_ref[here, :] = w[z].astype(BF16)
-    for c in started + [meta_move] + band_moves + g_moves:
+    for c in copies(pl.ds(0, n_dev - 1), t_recv, (), tile_peer(1)) + [meta_move, g_all] + band_moves:
         c.wait_send()
 
 
@@ -362,7 +357,6 @@
     n_rows = 2 * rows
     fields = 8 * p_dev + idx.size
     width = fields + -fields % LANES
-    chunk = 2 * LANES
     sem = pltpu.SemaphoreType.DMA
     return pl.pallas_call(
         functools.partial(focus_kernel, n_pulse, n_tile, r_dev),
@@ -380,7 +374,7 @@
             pltpu.VMEM((n_dev, 2 * p_dev, win), BF16),
             pltpu.VMEM((2, n_dev, 1, width), jnp.int32),
             pltpu.SMEM((n_dev, 1, width), jnp.int32),
-            pltpu.VMEM((ups // chunk, 2, win, chunk), BF16),
+            pltpu.VMEM(filt.shape, BF16),
             pltpu.VMEM((2, rows, win), BF16),
             pltpu.VMEM((rows * (ups // LANES) + 8, LANES), F32),
             pltpu.VMEM((rows * (band // LANES + 1), LANES), F32),
@@ -389,16 +383,15 @@
             pltpu.VMEM((n_tile, 2, n_rows), F32),
             pltpu.SemaphoreType.REGULAR,
             sem((6,)),
-            sem((ups // chunk,)),
             sem,
+            sem,
+            sem((2,)),
             sem((2, n_pulse)),
-            sem((2, n_pulse)),
-            sem((2, n_pulse, half)),
-            sem((2, n_pulse, half)),
+            sem((2,)),
             sem((3,)),
             sem((3,)),
-            sem((n_tile,)),
-            sem((n_tile,)),
+            sem,
+            sem,
         ],
         compiler_params=pltpu.CompilerParams(
             collective_id=0, has_side_effects=True, vmem_limit_bytes=VMEM_LIMIT
@@ -406,31 +399,26 @@
     )(*[pltpu.with_memory_space_constraint(a, pltpu.HBM) for a in (range_off, fine, dop, order, idx, raw, filt)])
 
 
-def image_kernel(left_ref, samp_ref, out_ref, res_ref, sem):
+def image_kernel(parts, left_ref, samp_ref, out_ref, res_ref, sem):
     r_dev = out_ref.shape[1]
-    parts = sem.shape[0]
     width = out_ref.shape[2] // parts
-    moves = []
     for i in range(parts):
         cols = pl.ds(i * width, width)
         res = jnp.dot(left_ref[...], samp_ref[:, cols], preferred_element_type=F32).astype(BF16)
         for z in range(2):
             res_ref[z, :, cols] = res[z * r_dev : (z + 1) * r_dev]
-        move = pltpu.make_async_copy(res_ref.at[:, :, cols], out_ref.at[:, :, cols], sem.at[i])
-        move.start()
-        moves.append(move)
-    for move in moves:
-        move.wait()
+        pltpu.make_async_copy(res_ref.at[:, :, cols], out_ref.at[:, :, cols], sem).start()
+    pltpu.make_async_copy(res_ref, out_ref, sem).wait()
 
 
 def image(left, samples, r_dev):
     cols = samples.shape[1]
     return pl.pallas_call(
-        image_kernel,
+        functools.partial(image_kernel, 8),
         out_shape=jax.ShapeDtypeStruct((2, r_dev, cols), BF16),
         in_specs=[pl.BlockSpec(memory_space=pltpu.VMEM)] * 2,
         out_specs=pl.BlockSpec(memory_space=pltpu.HBM),
-        scratch_shapes=[pltpu.VMEM((2, r_dev, cols), BF16), pltpu.SemaphoreType.DMA((8,))],
+        scratch_shapes=[pltpu.VMEM((2, r_dev, cols), BF16), pltpu.SemaphoreType.DMA],
         compiler_params=pltpu.CompilerParams(vmem_limit_bytes=IMAGE_VMEM),
     )(left, samples)
 

time: 21.7 us -> 20.8 us (0.959)
  Pallas kernels: 21.5 us -> 20.6 us
    pallas_call x1, Pallas kernels: 19.9 us -> 19 us  [focus(): pl.pallas_call(functools.partial(focus_kernel, n_pulse, n_tile, r_dev), o...]
where the time goes in v3:
time: 20.8 us; the launch traced here: 20.6 us
  Pallas kernels  20.6 us (99%)
    pallas_call x1, Pallas kernels, focus(): pl.pallas_call(functools.partial(focus_kernel, n_pulse, n_tile, r_dev), o...  19 us
    pallas_call x1, Pallas kernels, image(): pl.pallas_call(functools.partial(image_kernel, 8), out_shape=jax.ShapeDty...  1.55 us

profile of v3, /device:TPU:0, one launch (start us, length us, event | category | flops | bytes accessed | tf_op | source)
XLA Modules:
  0.0 20.6 jit_solution(10522596021591197306)
XLA Ops:
  0.0 19.0 %shard_map.73 = (bf16[256,256]{1,0:T(8,128)(2,1)S(1)}, bf16[256,4096]{1,0:T(8,128)(2,1)S(1)}) custom-call(s32[4]{0:T(128)} %off_in.1, s32[4]{0:T(128)} %fine_in.1, s32[4]{0:T(128)} %dop_in.1, s32[1,4]{1,0:T(1,128)} %order_in.1, s32[4,8]{1,0:T(4,128)} %bitcast.1, bf16[2,4,2048]{2,1,0:T(4,128)(2,1)} %raw_in.1, bf16[2,1024,2048]{2,1,0:T(8,128)(2,1)} %filt_ref.1), custom_call_target="tpu_custom_call" | custom-call | tf_op jit(solution)/shard_map/pallas_call | solution.py:361
  19.0 1.6 %shard_map.74 = bf16[2,128,4096]{2,1,0:T(8,128)(2,1)} custom-call(bf16[256,256]{1,0:T(8,128)(2,1)S(1)} %get-tuple-element.7.left_ref, bf16[256,4096]{1,0:T(8,128)(2,1)S(1)} %get-tuple-element.8.samp_ref), custom_call_target="tpu_custom_call" | custom-call | tf_op jit(solution)/shard_map/pallas_call | solution.py:416
